TPU v7x, 128 devices: a whole 4x4x4 slice. The times are simulated.
128 devices in a mesh: dp: 8 (over z, core), clus: 16 (over y, x).
Axes of the slice: x: 4, y: 4, z: 4, core: 2. Of those that a mesh axis runs over, the one named last changes fastest.
Arguments:
- points: bfloat16 [512, 128, 1024], P(('dp', 'clus')), may hold values from -40 to 40
- block_cluster: int32 [512, 1], P(('dp', 'clus')), may hold values from 0 to 255, as said below
- queries: bfloat16 [2048, 1024], P(('dp', 'clus')), may hold values from -6 to 6
- query_ids: int32 [256, 128], P(('dp', 'clus')), may hold values from 0 to 2047
Outputs:
- gram_tiles: float32 [256, 1024, 1024], P(('dp', 'clus'))
- cross: float32 [256, 1024, 128], P(('dp', 'clus'))
Inputs may be any that keep to these rules, and one draw needn't show every extreme that they name: `block_cluster`: cluster c is owned by the device at position c // 2 in the order of dp+clus, dp slowest. Of the 4 blocks of one device, at most 2 belong to clusters whose owners share one index along clus, exactly 2 for some device and index. Of all blocks on the devices of one index along dp, those whose owners share one index along clus number at most 3 for each owner index along dp, exactly 3 for some.
All inputs are finite; a program needn't handle non-finite values.
Results may differ from a plain program's by a relative error of at most 0.0022.
Values may be sent and summed in bfloat16 or wider, within the bound.
A program may use at most 128 MiB of HBM per device.

v0:
```python
import jax
import jax.numpy as jnp
from jax import lax
from jax.sharding import PartitionSpec as P

MEANROWS = 256


def rank_among(destination, live):
    count = destination.shape[0]
    row_pos = lax.broadcasted_iota(jnp.int32, (count, count), 0)
    col_pos = lax.broadcasted_iota(jnp.int32, (count, count), 1)
    same = (destination[:, None] == destination[None, :]) & (col_pos < row_pos) & live[None, :]
    return jnp.sum(same.astype(jnp.int32), axis=1)


def pack_slots(blocks, owners, live, destination, peers, capacity):
    rank = rank_among(destination, live)
    position = jnp.where(live, destination * capacity + rank, peers * capacity)
    slot_blocks = (
        jnp.zeros((peers * capacity,) + blocks.shape[1:], blocks.dtype)
        .at[position]
        .set(blocks, mode="drop")
    )
    slot_owner = jnp.full((peers * capacity,), -1, jnp.int32).at[position].set(owners, mode="drop")
    return (slot_blocks, slot_owner)


def block_terms(block, train_rows, width):
    squares = jnp.einsum("rd,rd->r", block, block, preferred_element_type=jnp.float32)
    row_weight = lax.rsqrt(squares / width + 1e-06)
    raw = jnp.einsum("md,rd->mr", train_rows, block, preferred_element_type=jnp.float32)
    scores = (raw * row_weight[None, :]).astype(jnp.bfloat16)
    gram_tile = jnp.einsum("ri,rj->ij", block, block, preferred_element_type=jnp.float32)
    cross_tile = jnp.einsum("ri,mr->im", block, scores, preferred_element_type=jnp.float32)
    return (gram_tile, cross_tile)


def local(points, block_cluster, queries, query_ids):
    n_clus = lax.axis_size("clus")
    n_dp = lax.axis_size("dp")
    nb_local, blk_rows, width = points.shape
    cl_own = query_ids.shape[0]
    mq_rows = query_ids.shape[1]
    owner_cap = 3 * ((nb_local + n_dp - 1) // n_dp)
    column_cap = (n_dp * owner_cap + n_clus - 1) // n_clus
    labels = block_cluster[:, 0]
    everywhere = jnp.ones((nb_local,), jnp.bool_)
    column = labels // cl_own % n_clus
    sent_blocks, sent_owner = pack_slots(points, labels, everywhere, column, n_clus, column_cap)
    mid_blocks, mid_owner = (
        lax.all_to_all(
            sent_blocks.reshape(n_clus, column_cap * blk_rows, width),
            "clus",
            split_axis=0,
            concat_axis=0,
            tiled=True,
        ),
        lax.all_to_all(
            sent_owner.reshape(n_clus, column_cap), "clus", split_axis=0, concat_axis=0, tiled=True
        ),
    )
    mid_blocks = mid_blocks.reshape(n_clus * column_cap, blk_rows, width)
    mid_owner = mid_owner.reshape(n_clus * column_cap)
    mid_live = mid_owner >= 0
    target_row = jnp.where(mid_live, mid_owner // cl_own // n_clus, 0)
    fwd_blocks, fwd_owner = pack_slots(mid_blocks, mid_owner, mid_live, target_row, n_dp, owner_cap)
    own_blocks, own_owner = (
        lax.all_to_all(
            fwd_blocks.reshape(n_dp, owner_cap * blk_rows, width),
            "dp",
            split_axis=0,
            concat_axis=0,
            tiled=True,
        ),
        lax.all_to_all(
            fwd_owner.reshape(n_dp, owner_cap), "dp", split_axis=0, concat_axis=0, tiled=True
        ),
    )
    slot_total = n_dp * owner_cap
    own_blocks = own_blocks.reshape(slot_total, blk_rows, width)
    own_owner = own_owner.reshape(slot_total)
    wanted = query_ids.reshape(cl_own * mq_rows)
    piece = lax.all_gather(queries, ("dp", "clus"), axis=0, tiled=True)
    inside = (wanted >= 0) & (wanted < piece.shape[0])
    rows = jnp.take(piece, jnp.clip(wanted, 0, piece.shape[0] - 1), axis=0)
    picked = jnp.where(inside[:, None], rows, jnp.zeros((cl_own * mq_rows, width), jnp.bfloat16))
    train = picked.reshape(cl_own, mq_rows, width)
    here = lax.axis_index("dp") * n_clus + lax.axis_index("clus")
    local_id = jnp.where(own_owner >= 0, own_owner - here * cl_own, cl_own).astype(jnp.int32)
    order = jnp.argsort(local_id, stable=True)
    cluster_pos = lax.broadcasted_iota(jnp.int32, (cl_own, slot_total), 0)
    counts = jnp.sum((local_id[None, :] == cluster_pos).astype(jnp.int32), axis=1)
    ends = jnp.cumsum(counts)
    starts = ends - counts
    factor = 1.0 / MEANROWS
    gram_list = []
    cross_list = []
    for owned in range(cl_own):
        train_rows = train[owned]

        def add_one(step, tiles):
            slot = order[step]
            block = lax.dynamic_index_in_dim(own_blocks, slot, 0, keepdims=False)
            gram_tile, cross_tile = block_terms(block, train_rows, width)
            return (tiles[0] + gram_tile, tiles[1] + cross_tile)

        gram_one, cross_one = lax.fori_loop(
            starts[owned],
            ends[owned],
            add_one,
            (jnp.zeros((width, width), jnp.float32), jnp.zeros((width, mq_rows), jnp.float32)),
        )
        gram_list.append(gram_one)
        cross_list.append(cross_one)
    gram_acc = jnp.stack(gram_list)
    cross_acc = jnp.stack(cross_list)
    return (gram_acc * factor, cross_acc * factor)


def solution(mesh):
    placed = (
        P(("dp", "clus"), None, None),
        P(("dp", "clus"), None),
        P(("dp", "clus"), None),
        P(("dp", "clus"), None),
    )
    return jax.shard_map(
        local,
        mesh=mesh,
        in_specs=placed,
        out_specs=(P(("dp", "clus"), None, None), P(("dp", "clus"), None, None)),
        check_vma=False,
    )
```

profile of v0, /device:TPU:53, one launch (start us, length us, event | category | flops | bytes accessed | tf_op | source)
XLA Modules:
  0.0 447.1 jit_solution(10070823107239796576)
XLA Ops:
  10.9 6.7 %all-to-all-start = ((s32[16,1,2]{2,1,0:T(1,128)}), s32[16,1,2]{2,1,0:T(1,128)S(1)}, u32[]{:S(2)}, u32[]{:S(2)}) async-start(s32[16,1,2]{2,1,0:T(1,128)} %bitcast.8), calls=%async_computation | async-start | bytes 16384 | tf_op jit(solution)/shard_map/all_to_all | solution.py:59
  17.5 4.5 broadcast_in_dim.61
  24.8 6.7 %all-to-all-start.2 = ((bf16[16,256,1024]{2,1,0:T(8,128)(2,1)}), bf16[16,256,1024]{2,1,0:T(8,128)(2,1)}, u32[]{:S(2)}, u32[]{:S(2)}) async-start(bf16[16,256,1024]{2,1,0:T(8,128)(2,1)} %bitcast.85), calls=%async_computation.2 | async-start | bytes 16777216 | tf_op jit(solution)/shard_map/all_to_all | solution.py:52
  35.1 115.8 %all-to-all-done.2 = bf16[16,256,1024]{2,1,0:T(8,128)(2,1)} async-done(((bf16[16,256,1024]{2,1,0:T(8,128)(2,1)}), bf16[16,256,1024]{2,1,0:T(8,128)(2,1)}, u32[]{:S(2)}, u32[]{:S(2)}) %all-to-all-start.2) | async-done | bytes 8388640 | tf_op jit(solution)/shard_map/all_to_all | solution.py:52
  151.0 7.4 %all-to-all-start.1 = ((s32[8,1,3]{2,1,0:T(1,128)}), s32[8,1,3]{2,1,0:T(1,128)S(1)}, u32[]{:S(2)}, u32[]{:S(2)}) async-start(s32[8,1,3]{2,1,0:T(1,128)} %bitcast.11), calls=%async_computation.1 | async-start | bytes 8192 | tf_op jit(solution)/shard_map/all_to_all | solution.py:76
  158.4 3.5 broadcast_in_dim.60
  161.9 16.4 %scatter_fusion.1 = bf16[24,128,1024]{2,1,0:T(8,128)(2,1)} fusion(bf16[24,128,1024]{2,1,0:T(8,128)(2,1)} %broadcast_in_dim.60, s32[32]{0:T(128)S(1)} %fusion.34, bf16[32,128,1024]{2,1,0:T(8,128)(2,1)} %bitcast.17), kind=kCustom, calls=%fused_computation.4 | custom fusion | bytes 25165952 | tf_op jit(solution)/shard_map/scatter | solution.py:23
  178.3 9.5 %all-to-all-start.3 = ((bf16[8,384,1024]{2,1,0:T(8,128)(2,1)}), bf16[8,384,1024]{2,1,0:T(8,128)(2,1)}, u32[]{:S(2)}, u32[]{:S(2)}) async-start(bf16[8,384,1024]{2,1,0:T(8,128)(2,1)} %bitcast.84), calls=%async_computation.3 | async-start | bytes 12582912 | tf_op jit(solution)/shard_map/all_to_all | solution.py:69
  191.2 4.3 gather_fusion
  195.7 62.4 %all-to-all-done.3 = bf16[8,384,1024]{2,1,0:T(8,128)(2,1)} async-done(((bf16[8,384,1024]{2,1,0:T(8,128)(2,1)}), bf16[8,384,1024]{2,1,0:T(8,128)(2,1)}, u32[]{:S(2)}, u32[]{:S(2)}) %all-to-all-start.3) | async-done | bytes 6291488 | tf_op jit(solution)/shard_map/all_to_all | solution.py:69
  260.8 45.4 %while.24 = (s32[]{:T(128)}, f32[1024,1024]{1,0:T(8,128)}, f32[1024,128]{1,0:T(8,128)S(1)}, s32[]{:T(128)}, s32[24]{0:T(128)S(1)}, /*index=5*/bf16[24,128,1024]{...) while((s32[]{:T(128)}, f32[1024,1024]{1,0:T(8,128)}, ...), condition=%wide.region_10.11_spmd, body=%wide.region_9.10_spmd.sunk | while | flops 337150080 | bytes 10751165 | solution.py:108
  266.5 5.2 %convolution_add_fusion.8 = f32[1024,1024]{1,0:T(8,128)} fusion(f32[1024,1024]{1,0:T(8,128)} %get-tuple-element.249, bf16[24,128,1024]{2,1,0:T(8,128)(2,1)} %get-tuple-element.263, s32[]{:T(128)S(6)} %select_n.248), kind=kOutput, calls=%fused_computation.5.clone.1 | convolution fusion | flops 269484032 | bytes 8650756 | tf_op jit(solution)/shard_map/while/body/ri,rj->ij/dot_general | solution.py:34
  281.2 5.2 %convolution_add_fusion.8 = f32[1024,1024]{1,0:T(8,128)} fusion(f32[1024,1024]{1,0:T(8,128)} %get-tuple-element.249, bf16[24,128,1024]{2,1,0:T(8,128)(2,1)} %get-tuple-element.263, s32[]{:T(128)S(6)} %select_n.248), kind=kOutput, calls=%fused_computation.5.clone.1 | convolution fusion | flops 269484032 | bytes 8650756 | tf_op jit(solution)/shard_map/while/body/ri,rj->ij/dot_general | solution.py:34
  295.9 5.2 %convolution_add_fusion.8 = f32[1024,1024]{1,0:T(8,128)} fusion(f32[1024,1024]{1,0:T(8,128)} %get-tuple-element.249, bf16[24,128,1024]{2,1,0:T(8,128)(2,1)} %get-tuple-element.263, s32[]{:T(128)S(6)} %select_n.248), kind=kOutput, calls=%fused_computation.5.clone.1 | convolution fusion | flops 269484032 | bytes 8650756 | tf_op jit(solution)/shard_map/while/body/ri,rj->ij/dot_general | solution.py:34
  308.7 121.6 %while.25 = (s32[]{:T(128)}, f32[1024,1024]{1,0:T(8,128)}, f32[1024,128]{1,0:T(8,128)S(1)}, s32[]{:T(128)}, s32[24]{0:T(128)S(1)}, /*index=5*/bf16[24,128,1024]{...) while((s32[]{:T(128)}, f32[1024,1024]{1,0:T(8,128)}, ...), condition=%wide.region_12.13_spmd, body=%wide.region_11.12_spmd.sunk | while | flops 337150080 | bytes 10751165 | solution.py:108
  314.7 5.1 %convolution_add_fusion.10 = f32[1024,1024]{1,0:T(8,128)} fusion(f32[1024,1024]{1,0:T(8,128)} %get-tuple-element.219, bf16[24,128,1024]{2,1,0:T(8,128)(2,1)} %get-tuple-element.233, s32[]{:T(128)S(6)} %select_n.250), kind=kOutput, calls=%fused_computation.19.clone.1 | convolution fusion | flops 269484032 | bytes 8650756 | tf_op jit(solution)/shard_map/while/body/ri,rj->ij/dot_general | solution.py:34
  329.7 5.1 %convolution_add_fusion.10 = f32[1024,1024]{1,0:T(8,128)} fusion(f32[1024,1024]{1,0:T(8,128)} %get-tuple-element.219, bf16[24,128,1024]{2,1,0:T(8,128)(2,1)} %get-tuple-element.233, s32[]{:T(128)S(6)} %select_n.250), kind=kOutput, calls=%fused_computation.19.clone.1 | convolution fusion | flops 269484032 | bytes 8650756 | tf_op jit(solution)/shard_map/while/body/ri,rj->ij/dot_general | solution.py:34
  344.8 5.1 %convolution_add_fusion.10 = f32[1024,1024]{1,0:T(8,128)} fusion(f32[1024,1024]{1,0:T(8,128)} %get-tuple-element.219, bf16[24,128,1024]{2,1,0:T(8,128)(2,1)} %get-tuple-element.233, s32[]{:T(128)S(6)} %select_n.250), kind=kOutput, calls=%fused_computation.19.clone.1 | convolution fusion | flops 269484032 | bytes 8650756 | tf_op jit(solution)/shard_map/while/body/ri,rj->ij/dot_general | solution.py:34
  359.8 5.1 %convolution_add_fusion.10 = f32[1024,1024]{1,0:T(8,128)} fusion(f32[1024,1024]{1,0:T(8,128)} %get-tuple-element.219, bf16[24,128,1024]{2,1,0:T(8,128)(2,1)} %get-tuple-element.233, s32[]{:T(128)S(6)} %select_n.250), kind=kOutput, calls=%fused_computation.19.clone.1 | convolution fusion | flops 269484032 | bytes 8650756 | tf_op jit(solution)/shard_map/while/body/ri,rj->ij/dot_general | solution.py:34
  374.8 5.1 %convolution_add_fusion.10 = f32[1024,1024]{1,0:T(8,128)} fusion(f32[1024,1024]{1,0:T(8,128)} %get-tuple-element.219, bf16[24,128,1024]{2,1,0:T(8,128)(2,1)} %get-tuple-element.233, s32[]{:T(128)S(6)} %select_n.250), kind=kOutput, calls=%fused_computation.19.clone.1 | convolution fusion | flops 269484032 | bytes 8650756 | tf_op jit(solution)/shard_map/while/body/ri,rj->ij/dot_general | solution.py:34
  389.9 5.1 %convolution_add_fusion.10 = f32[1024,1024]{1,0:T(8,128)} fusion(f32[1024,1024]{1,0:T(8,128)} %get-tuple-element.219, bf16[24,128,1024]{2,1,0:T(8,128)(2,1)} %get-tuple-element.233, s32[]{:T(128)S(6)} %select_n.250), kind=kOutput, calls=%fused_computation.19.clone.1 | convolution fusion | flops 269484032 | bytes 8650756 | tf_op jit(solution)/shard_map/while/body/ri,rj->ij/dot_general | solution.py:34
  404.9 5.1 %convolution_add_fusion.10 = f32[1024,1024]{1,0:T(8,128)} fusion(f32[1024,1024]{1,0:T(8,128)} %get-tuple-element.219, bf16[24,128,1024]{2,1,0:T(8,128)(2,1)} %get-tuple-element.233, s32[]{:T(128)S(6)} %select_n.250), kind=kOutput, calls=%fused_computation.19.clone.1 | convolution fusion | flops 269484032 | bytes 8650756 | tf_op jit(solution)/shard_map/while/body/ri,rj->ij/dot_general | solution.py:34
  420.0 5.1 %convolution_add_fusion.10 = f32[1024,1024]{1,0:T(8,128)} fusion(f32[1024,1024]{1,0:T(8,128)} %get-tuple-element.219, bf16[24,128,1024]{2,1,0:T(8,128)(2,1)} %get-tuple-element.233, s32[]{:T(128)S(6)} %select_n.250), kind=kOutput, calls=%fused_computation.19.clone.1 | convolution fusion | flops 269484032 | bytes 8650756 | tf_op jit(solution)/shard_map/while/body/ri,rj->ij/dot_general | solution.py:34
  431.4 8.8 %maximum_multiply_fusion = f32[2,1024,1024]{2,1,0:T(8,128)} fusion(f32[1,1024,1024]{2,1,0:T(8,128)} %bitcast.82, f32[1,1024,1024]{2,1,0:T(8,128)} %bitcast.83), kind=kLoop, calls=%fused_computation.33 | loop fusion | flops 4194304 | bytes 16777216 | tf_op jit(solution)/shard_map/mul | solution.py:118
  (91 shorter events, 55.8 us)
Async XLA Ops:
  7.2 14.8 %copy-start = (bf16[4,128,1024]{2,1,0:T(8,128)(2,1)S(1)}, bf16[4,128,1024]{2,1,0:T(8,128)(2,1)}, u32[]{:S(2)}) copy-start(bf16[4,128,1024]{2,1,0:T(8,128)(2,1)} %param.8) | copy-start | bytes 3145732
  10.9 13.9 %all-to-all-start = ((s32[16,1,2]{2,1,0:T(1,128)}), s32[16,1,2]{2,1,0:T(1,128)S(1)}, u32[]{:S(2)}, u32[]{:S(2)}) async-start(s32[16,1,2]{2,1,0:T(1,128)} %bitcast.8), calls=%async_computation | async-start | bytes 16384 | tf_op jit(solution)/shard_map/all_to_all | solution.py:59
  24.8 126.2 %all-to-all-start.2 = ((bf16[16,256,1024]{2,1,0:T(8,128)(2,1)}), bf16[16,256,1024]{2,1,0:T(8,128)(2,1)}, u32[]{:S(2)}, u32[]{:S(2)}) async-start(bf16[16,256,1024]{2,1,0:T(8,128)(2,1)} %bitcast.85), calls=%async_computation.2 | async-start | bytes 16777216 | tf_op jit(solution)/shard_map/all_to_all | solution.py:52
  31.4 159.8 %all-gather.2.cloned.1.call-start = ((), (), s32[]{:S(2)}) async-start(), calls=%async_computation.4 | async-start | bytes 4227072 | tf_op jit(solution)/shard_map/all_gather | solution.py:84
  151.0 27.3 %all-to-all-start.1 = ((s32[8,1,3]{2,1,0:T(1,128)}), s32[8,1,3]{2,1,0:T(1,128)S(1)}, u32[]{:S(2)}, u32[]{:S(2)}) async-start(s32[8,1,3]{2,1,0:T(1,128)} %bitcast.11), calls=%async_computation.1 | async-start | bytes 8192 | tf_op jit(solution)/shard_map/all_to_all | solution.py:76
  178.3 9.5 %copy-start.1 = (s32[2,128]{1,0:T(2,128)S(1)}, s32[2,128]{1,0:T(2,128)}, u32[]{:S(2)}) copy-start(s32[2,128]{1,0:T(2,128)} %param.11) | copy-start | bytes 3076
  178.3 79.8 %all-to-all-start.3 = ((bf16[8,384,1024]{2,1,0:T(8,128)(2,1)}), bf16[8,384,1024]{2,1,0:T(8,128)(2,1)}, u32[]{:S(2)}, u32[]{:S(2)}) async-start(bf16[8,384,1024]{2,1,0:T(8,128)(2,1)} %bitcast.84), calls=%async_computation.3 | async-start | bytes 12582912 | tf_op jit(solution)/shard_map/all_to_all | solution.py:69
Sparse Core Ops, SparseCore 0:
  35.4 143.7 all-gather.1
where the time goes:
time: 449 us; the launch traced here: 447 us
  waiting for transfers between devices  179 us (40%)
  loops' own time  74.6 us (17%)
  matrix products  74 us (16%)
  local copies, waits for them, and re-layouts  48 us (11%)
  starting transfers between devices  30.3 us (7%)
  other arithmetic  27.1 us (6%)
  between operations  14.2 us (3%)
    all_to_all x1, waiting for transfers between devices, local(): lax.all_to_all(sent_blocks.reshape(n_clus, column_cap * blk_rows, width),...  116 us
    another operation x2, loops' own time, local(): lax.fori_loop(starts[owned], ends[owned], add_one, (jnp.zeros((width, wid...  74.6 us
    all_to_all x1, waiting for transfers between devices, local(): lax.all_to_all(fwd_blocks.reshape(n_dp, owner_cap * blk_rows, width), 'dp...  62.4 us
    dot_general x11, matrix products, block_terms(): jnp.einsum('ri,rj->ij', block, block, preferred_element_type=jnp.float32)  56.6 us
    scatter x2, local copies, waits for them, and re-layouts, pack_slots(): slot_blocks = jnp.zeros((peers * capacity,) + blocks.shape[1:], blocks.dt...  19.2 us
    dot_general x11, matrix products, block_terms(): jnp.einsum('ri,mr->im', block, scores, preferred_element_type=jnp.float32)  17.4 us
    dot_general x11, other arithmetic, block_terms(): jnp.einsum('rd,rd->r', block, block, preferred_element_type=jnp.float32)  11.9 us
    mul x2, other arithmetic, local(): return (gram_acc * factor, cross_acc * factor)  9.82 us
  transfers between devices with their start and end apart: 5, of which 2 were waited for; matrix products, arithmetic and copies ran while one was open for 8% of the time, Pallas kernels for 0%

commit v1 on v0

v1 whole, which is shorter than its diff:
```python
import functools

import jax
import jax.numpy as jnp
from jax import lax
from jax.experimental import pallas as pl
from jax.experimental.pallas import tpu as pltpu
from jax.sharding import PartitionSpec as P

MEANROWS = 256
MESH = pl.DeviceIdType.MESH
RING = 4
MID_CAP = 8
OWN_CAP = 3
ROWS = 16
COL_SPLIT = 2


def one_hot_pick(values, mask, rank, count):
    slot = lax.broadcasted_iota(jnp.int32, (count,) + mask.shape, 0)
    hit = mask[None] & (rank[None] == slot)
    return jnp.sum(jnp.where(hit, values, 0), axis=-1)


def before(mask):
    n = mask.shape[-1]
    row = lax.broadcasted_iota(jnp.int32, (n, n), 0)
    col = lax.broadcasted_iota(jnp.int32, (n, n), 1)
    return jnp.sum((mask[..., None, :] & (col < row)).astype(jnp.int32), axis=-1)


def tables(labels, dp, cl, cl_own, n_dp, n_clus, nb):
    y, x = cl // RING, cl % RING
    per_row = n_clus * nb
    row = lax.dynamic_index_in_dim(labels, dp, 0, keepdims=False)
    col = row // cl_own % n_clus
    dest = row // cl_own // n_clus
    grid = col.reshape(RING, RING, nb)
    pos = jnp.arange(RING, dtype=jnp.int32)
    local = jnp.arange(RING * nb, dtype=jnp.int32)
    ring_x = lax.dynamic_index_in_dim(grid, y, 0, keepdims=False).reshape(RING * nb)
    ring_y = lax.dynamic_index_in_dim(grid, x, 1, keepdims=False).reshape(RING * nb)
    mask_a = ring_x[None, :] == (pos * RING + x)[:, None]
    mask_b = ring_y[None, :] == (y * RING + pos)[:, None]
    pick_a = one_hot_pick(local, mask_a, before(mask_a), MID_CAP).T
    pick_b = one_hot_pick(local, mask_b, before(mask_b), MID_CAP).T
    mine = grid == cl
    mine_a = mine.reshape(RING, RING * nb)
    mine_b = mine.transpose(1, 0, 2).reshape(RING, RING * nb)
    at_a = (before(mine_a) + pos[:, None] * MID_CAP).reshape(per_row)
    at_b = (before(mine_b) + pos[:, None] * MID_CAP).reshape(RING, RING, nb).transpose(1, 0, 2).reshape(per_row)
    to_row = mine.reshape(1, per_row) & (dest[None, :] == jnp.arange(n_dp, dtype=jnp.int32)[:, None])
    rank = before(to_row)
    send_a = one_hot_pick(at_a, to_row, rank, OWN_CAP).T
    send_b = one_hot_pick(at_b, to_row, rank, OWN_CAP).T
    route = jnp.concatenate([t.reshape(-1) for t in (pick_a, pick_b, send_a, send_b)]).astype(jnp.int32)
    here = dp * n_clus + cl
    owned = labels // cl_own == here
    rank_all = before(owned)
    slot_local = one_hot_pick(labels % cl_own + 1, owned, rank_all, OWN_CAP).T.reshape(-1) - 1
    return route, slot_local


def place_slots(slot_local, cl_own):
    position = jnp.full(slot_local.shape, -1, jnp.int32)
    base = jnp.zeros((), jnp.int32)
    counts, bases = [], []
    for owned in range(cl_own):
        mask = slot_local == owned
        count = jnp.sum(mask.astype(jnp.int32))
        position = jnp.where(mask, base + before(mask), position)
        counts.append(count)
        bases.append(base)
        base = base + (count + 1) // 2 * 2
    return jnp.concatenate([position, jnp.stack(counts + bases)]).astype(jnp.int32)


def route_kernel(nb, blk, width, n_dp, tab, pts, out, *scratch):
    pieces = []
    half = blk // 2
    wide = width // COL_SPLIT
    for row0 in range(0, half, ROWS):
        for c0 in range(0, width, wide):
            pieces.append((row0, c0))
    steps = len(pieces)
    total = 2 * steps
    got1, pack2, got2, pack3 = (scratch[i * total:(i + 1) * total] for i in range(4))
    s1, r1, s2, r2, s3, r3, own = scratch[4 * total:]
    dp = lax.axis_index("dp")
    cl = lax.axis_index("clus")
    y, x = lax.div(cl, RING), lax.rem(cl, RING)

    def peer(cls, stage, delta):
        along_x = (cls == 0) == (stage == 1)
        if along_x:
            at = lax.rem(x + delta, RING)
            return at, (dp, y * RING + at)
        at = lax.rem(y + delta, RING)
        return at, (dp, at * RING + x)

    def row_peer(delta):
        at = lax.rem(dp + delta, n_dp)
        return at, (at, cl)

    barrier = pltpu.get_barrier_semaphore()
    friends = [peer(cls, 1, d)[1] for cls in (0, 1) for d in range(1, RING)]
    friends += [row_peer(d)[1] for d in range(1, n_dp)]
    for friend in friends:
        pl.semaphore_signal(barrier, inc=1, device_id=friend, device_id_type=MESH)
    pl.semaphore_wait(barrier, len(friends))

    def spot(step, cls):
        row0, c0 = pieces[step]
        return pl.ds(row0 + cls * half, ROWS), pl.ds(c0, wide)

    def copies1(step, cls):
        q = 2 * step + cls
        rows, cols = spot(step, cls)
        me = x if cls == 0 else y
        return [
            pltpu.make_async_remote_copy(
                src_ref=pts.at[:, rows, cols],
                dst_ref=got1[q].at[pl.ds(me * nb, nb)],
                send_sem=s1.at[q, d - 1],
                recv_sem=r1.at[q, d - 1],
                device_id=peer(cls, 1, d)[1],
                device_id_type=MESH,
            )
            for d in range(1, RING)
        ]

    def copies2(step, cls):
        q = 2 * step + cls
        me = y if cls == 0 else x
        made = []
        for d in range(1, RING):
            at, device = peer(cls, 2, d)
            made.append(
                pltpu.make_async_remote_copy(
                    src_ref=pack2[q].at[pl.ds(at * MID_CAP, MID_CAP)],
                    dst_ref=got2[q].at[pl.ds(me * MID_CAP, MID_CAP)],
                    send_sem=s2.at[q, d - 1],
                    recv_sem=r2.at[q, d - 1],
                    device_id=device,
                    device_id_type=MESH,
                )
            )
        return made

    def copies3(step, cls):
        q = 2 * step + cls
        rows, cols = spot(step, cls)
        made = []
        for d in range(1, n_dp):
            at, device = row_peer(d)
            made.append(
                pltpu.make_async_remote_copy(
                    src_ref=pack3[q].at[pl.ds(at * OWN_CAP, OWN_CAP)],
                    dst_ref=out.at[pl.ds(dp * OWN_CAP, OWN_CAP), rows, cols],
                    send_sem=s3.at[q, d - 1],
                    recv_sem=r3.at[q, d - 1],
                    device_id=device,
                    device_id_type=MESH,
                )
            )
        return made

    def own_copy(step, cls):
        q = 2 * step + cls
        rows, cols = spot(step, cls)
        return pltpu.make_async_copy(
            pack3[q].at[pl.ds(dp * OWN_CAP, OWN_CAP)], out.at[pl.ds(dp * OWN_CAP, OWN_CAP), rows, cols], own.at[q]
        )

    def start1(step):
        for cls in (0, 1):
            for copy in copies1(step, cls):
                copy.start()

    def step12(step):
        for cls in (0, 1):
            q = 2 * step + cls
            rows, cols = spot(step, cls)
            me = x if cls == 0 else y
            mid = y if cls == 0 else x
            got1[q][pl.ds(me * nb, nb)] = pts[:, rows, cols]
            for copy in copies1(step, cls):
                copy.wait_recv()

            def pack(k, carry, q=q, cls=cls):
                pack2[q][k] = got1[q][tab[cls * RING * MID_CAP + k]]
                return carry

            lax.fori_loop(0, RING * MID_CAP, pack, 0, unroll=8)
            for copy in copies2(step, cls):
                copy.start()
            got2[q][pl.ds(mid * MID_CAP, MID_CAP)] = pack2[q][pl.ds(mid * MID_CAP, MID_CAP)]

    def step23(step):
        for cls in (0, 1):
            q = 2 * step + cls
            for copy in copies2(step, cls):
                copy.wait_recv()
            base = 2 * RING * MID_CAP + cls * n_dp * OWN_CAP

            def pack(k, carry, q=q, base=base):
                pack3[q][k] = got2[q][tab[base + k]]
                return carry

            lax.fori_loop(0, n_dp * OWN_CAP, pack, 0, unroll=8)
            for copy in copies3(step, cls):
                copy.start()
            own_copy(step, cls).start()

    start1(0)
    start1(1)
    for step in range(steps + 1):
        if step < steps:
            step12(step)
            if step + 2 < steps:
                start1(step + 2)
        if step >= 1:
            step23(step - 1)
    for step in range(steps):
        for cls in (0, 1):
            for copy in copies1(step, cls) + copies2(step, cls):
                copy.wait_send()
            for copy in copies3(step, cls):
                copy.wait()
            own_copy(step, cls).wait()


def route(points, table, n_dp):
    nb, blk, width = points.shape
    total = 2 * (blk // 2 // ROWS) * COL_SPLIT
    wide = width // COL_SPLIT
    kind = points.dtype

    def many(count):
        return [pltpu.VMEM((count, ROWS, wide), kind) for _ in range(total)]

    return pl.pallas_call(
        functools.partial(route_kernel, nb, blk, width, n_dp),
        out_shape=jax.ShapeDtypeStruct((n_dp * OWN_CAP, blk, width), kind),
        in_specs=[pl.BlockSpec(memory_space=pltpu.SMEM), pl.BlockSpec(memory_space=pltpu.VMEM)],
        out_specs=pl.BlockSpec(memory_space=pl.ANY),
        scratch_shapes=many(RING * nb) + many(RING * MID_CAP) * 2 + many(n_dp * OWN_CAP)
        + [pltpu.SemaphoreType.DMA((total, RING - 1))] * 4
        + [pltpu.SemaphoreType.DMA((total, n_dp - 1))] * 2
        + [pltpu.SemaphoreType.DMA((total,))],
        compiler_params=pltpu.CompilerParams(
            collective_id=0, has_side_effects=True, vmem_limit_bytes=60 * 1024 * 1024
        ),
        name="route",
    )(table, points)


def product_kernel(slots, cl_own, blk, tile, factor, place, blocks, train, gram, cross, sorted_blocks, scores, sem):
    group = pl.program_id(0)
    part = pl.program_id(1)
    step_rows = 2 * blk

    def fetch(k):
        at = place[k]
        return at, pltpu.make_async_copy(blocks.at[k], sorted_blocks.at[pl.ds(pl.multiple_of(at * blk, blk), blk)], sem.at[k])

    @pl.when((group == 0) & (part == 0))
    def _():
        def begin(k, carry):
            @pl.when(place[k] >= 0)
            def _():
                fetch(k)[1].start()
            return carry

        lax.fori_loop(0, slots, begin, 0)
        for owned in range(cl_own):
            count = place[slots + owned]
            end = place[slots + cl_own + owned] + count

            @pl.when(lax.rem(count, 2) == 1)
            def _():
                sorted_blocks[pl.ds(pl.multiple_of(end * blk, blk), blk), :] = jnp.zeros(
                    (blk, sorted_blocks.shape[1]), sorted_blocks.dtype
                )

        def finish(k, carry):
            @pl.when(place[k] >= 0)
            def _():
                fetch(k)[1].wait()
            return carry

        lax.fori_loop(0, slots, finish, 0)

    count = place[slots + group]
    base = place[slots + cl_own + group]
    steps = lax.div(count + 1, 2)

    def rows_of(step):
        return pl.ds(pl.multiple_of((base + 2 * step) * blk, blk), step_rows)

    @pl.when(part == 0)
    def _():
        def score(step, carry):
            rows = sorted_blocks[rows_of(step), :]
            wide = rows.astype(jnp.float32)
            weight = lax.rsqrt(jnp.mean(wide * wide, axis=1, keepdims=True) + 1e-06)
            raw = lax.dot_general(rows, train[0], (((1,), (1,)), ((), ())), preferred_element_type=jnp.float32)
            scores[pl.ds(pl.multiple_of(step * step_rows, step_rows), step_rows), :] = (raw * weight).astype(scores.dtype)
            return carry

        lax.fori_loop(0, steps, score, 0)

    columns = pl.ds(pl.multiple_of(part * tile, tile), tile)

    def terms(step):
        rows = rows_of(step)
        left = sorted_blocks[rows, columns]
        contract = (((0,), (0,)), ((), ()))
        a = lax.dot_general(left, sorted_blocks[rows, :], contract, preferred_element_type=jnp.float32)
        part_scores = scores[pl.ds(pl.multiple_of(step * step_rows, step_rows), step_rows), :]
        b = lax.dot_general(left, part_scores, contract, preferred_element_type=jnp.float32)
        return a * factor, b * factor

    @pl.when(count == 0)
    def _():
        gram[...] = jnp.zeros_like(gram)
        cross[...] = jnp.zeros_like(cross)

    @pl.when(count > 0)
    def _():
        a, b = terms(0)
        gram[0] = a
        cross[0] = b

        def add(step, carry):
            a, b = terms(step)
            gram[0] += a
            cross[0] += b
            return carry

        lax.fori_loop(1, steps, add, 0)


def products(blocks, place, train):
    slots, blk, width = blocks.shape
    cl_own, mq, _ = train.shape
    tile = 256
    return pl.pallas_call(
        functools.partial(product_kernel, slots, cl_own, blk, tile, 1.0 / MEANROWS),
        out_shape=(
            jax.ShapeDtypeStruct((cl_own, width, width), jnp.float32),
            jax.ShapeDtypeStruct((cl_own, width, mq), jnp.float32),
        ),
        grid_spec=pltpu.PrefetchScalarGridSpec(
            num_scalar_prefetch=1,
            grid=(cl_own, width // tile),
            in_specs=[
                pl.BlockSpec(memory_space=pl.ANY),
                pl.BlockSpec((1, mq, width), lambda g, i, place: (g, 0, 0)),
            ],
            out_specs=(
                pl.BlockSpec((1, tile, width), lambda g, i, place: (g, i, 0)),
                pl.BlockSpec((1, tile, mq), lambda g, i, place: (g, i, 0)),
            ),
            scratch_shapes=[
                pltpu.VMEM(((slots + cl_own) * blk, width), blocks.dtype),
                pltpu.VMEM(((slots + 2) * blk, mq), blocks.dtype),
                pltpu.SemaphoreType.DMA((slots,)),
            ],
        ),
        compiler_params=pltpu.CompilerParams(
            dimension_semantics=("arbitrary", "arbitrary"), vmem_limit_bytes=40 * 1024 * 1024
        ),
        name="products",
    )(place, blocks, train)


def local(points, block_cluster, queries, query_ids):
    n_clus = lax.axis_size("clus")
    n_dp = lax.axis_size("dp")
    dp = lax.axis_index("dp")
    cl = lax.axis_index("clus")
    nb, _, width = points.shape
    cl_own, mq = query_ids.shape
    labels = lax.all_gather(block_cluster[:, 0], ("dp", "clus"), axis=0, tiled=True).reshape(n_dp, n_clus * nb)
    table, slot_local = tables(labels, dp, cl, cl_own, n_dp, n_clus, nb)
    place = place_slots(slot_local, cl_own)
    all_queries = lax.all_gather(queries, ("dp", "clus"), axis=0, tiled=True)
    own_blocks = route(points, table, n_dp)
    train = jnp.take(all_queries, query_ids.reshape(cl_own * mq), axis=0, mode="clip").reshape(cl_own, mq, width)
    return products(own_blocks, place, train)


def solution(mesh):
    placed = (
        P(("dp", "clus"), None, None),
        P(("dp", "clus"), None),
        P(("dp", "clus"), None),
        P(("dp", "clus"), None),
    )
    return jax.shard_map(
        local,
        mesh=mesh,
        in_specs=placed,
        out_specs=(P(("dp", "clus"), None, None), P(("dp", "clus"), None, None)),
        check_vma=False,
    )
```

time: 449 us -> 200 us (0.45)
  the two profiles are of different devices: /device:TPU:53 before, /device:TPU:3 now
where the time goes in v1:
time: 200 us; the launch traced here: 197 us
  Pallas kernels  100 us (50%)
  blocking collectives  67.3 us (34%)
  between operations  14.9 us (7%)
  local copies, waits for them, and re-layouts  10.9 us (5%)
  other arithmetic  3.1 us (2%)
    pallas_call x1, Pallas kernels, route(): pl.pallas_call(functools.partial(route_kernel, nb, blk, width, n_dp), out...  91 us
    unnamed x1, blocking collectives  67.3 us
    pallas_call x1, Pallas kernels, products(): pl.pallas_call(functools.partial(product_kernel, slots, cl_own, blk, tile...  9.19 us
    gather x1, local copies, waits for them, and re-layouts, local(): jnp.take(all_queries, query_ids.reshape(cl_own * mq), axis=0, mode='clip')  4.28 us
  transfers between devices with their start and end apart: 1, of which 0 were waited for; matrix products, arithmetic and copies ran while one was open for 4% of the time, Pallas kernels for 46%

profile of v1, /device:TPU:3, one launch (start us, length us, event | category | flops | bytes accessed | tf_op | source)
XLA Modules:
  0.0 197.1 jit_solution(6951513544288046192)
XLA Ops:
  7.2 0.7 all-gather.3.cloned.1.call-update
  8.0 0.8 bitcast_dynamic-update-slice_fusion
  8.7 67.3 %all-reduce = s32[512]{0:T(512)S(1)} all-reduce(s32[512]{0:T(512)S(1)} %bitcast_dynamic-update-slice_fusion), channel_id=2, replica_groups=mesh['dp'=8,'clus'=16] {'dp','clus'}, use_global_device_ids=true, to_apply=%add | all-reduce | flops 512 | bytes 4096
  76.2 0.1 squeeze.14
  76.3 0.1 and.278
  76.4 0.1 eq.184
  76.8 0.4 convert_reduce_fusion.5
  77.5 0.1 reshape.377
  77.7 0.3 convert_reduce_fusion
  78.1 0.3 select_reduce_fusion.3
  78.3 0.6 convert_reduce_fusion.9
  79.6 0.2 select_reduce_fusion
  80.3 0.1 copy.10
  80.4 0.1 eq.180
  80.5 0.1 copy.11
  80.6 0.1 eq.183
  80.7 0.6 pad_add_fusion.tab
  81.3 91.0 %route.1.blocks = bf16[24,128,1024]{2,1,0:T(8,128)(2,1)} custom-call(s32[112]{0:T(128)} %pad_add_fusion.tab, bf16[4,128,1024]{2,1,0:T(8,128)(2,1)} %pts.1), custom_call_target="tpu_custom_call" | custom-call | tf_op jit(solution)/shard_map/route/pallas_call | solution.py:242
  172.4 0.1 convert_reduce_fusion.7
  172.5 0.1 convert_reduce_fusion.6
  172.6 1.4 concatenate.6.place
  174.0 4.3 %gather_fusion = bf16[256,1024]{1,0:T(8,128)(2,1)S(1)} fusion(bf16[2048,1024]{1,0:T(8,128)(2,1)} %all-gather.3.cloned.1.call-done, s32[1024]{0:T(1024)S(1)} %pad_clamp_fusion), kind=kCustom, calls=%fused_computation | custom fusion | bytes 1049600 | tf_op jit(solution)/shard_map/jit(_take)/gather | solution.py:390
  178.3 2.8 %copy-done = bf16[24,128,1024]{2,1,0:T(8,128)(2,1)S(1)} copy-done((bf16[24,128,1024]{2,1,0:T(8,128)(2,1)S(1)}, bf16[24,128,1024]{2,1,0:T(8,128)(2,1)}, u32[]{:S(2)}) %copy-start) | copy-done | bytes 6291480
  181.1 9.2 %products.1 = (f32[2,1024,1024]{2,1,0:T(8,128)}, f32[2,1024,128]{2,1,0:T(8,128)}) custom-call(s32[28]{0:T(128)S(1)} %concatenate.6.place, bf16[24,128,1024]{2,1,0:T(8,128)(2,1)S(1)} %copy-done, bf16[2,128,1024]{2,1,0:T(8,128)(2,1)S(1)} %bitcast.23), custom_call_target="tpu_custom_call" | custom-call | tf_op jit(solution)/shard_map/products/pallas_call | solution.py:348
  (40 shorter events, 1.5 us)
Async XLA Ops:
  7.2 166.8 %copy-start.1 = (s32[2,128]{1,0:T(2,128)S(1)}, s32[2,128]{1,0:T(2,128)}, u32[]{:S(2)}) copy-start(s32[2,128]{1,0:T(2,128)} %param.7) | copy-start | bytes 3076
  7.2 166.8 %all-gather.3.cloned.1.call-start = ((), (), s32[]{:S(2)}) async-start(), calls=%async_computation | async-start | bytes 4227072 | tf_op jit(solution)/shard_map/all_gather | solution.py:388
  178.3 2.8 %copy-start = (bf16[24,128,1024]{2,1,0:T(8,128)(2,1)S(1)}, bf16[24,128,1024]{2,1,0:T(8,128)(2,1)}, u32[]{:S(2)}) copy-start(bf16[24,128,1024]{2,1,0:T(8,128)(2,1)} %route.1.blocks) | copy-start | bytes 18874372
Sparse Core Ops, SparseCore 0:
  11.1 68.3 all-gather.2

commit v2 on v1

v2 whole, which is shorter than its diff:
```python
import functools

import jax
import jax.numpy as jnp
from jax import lax
from jax.experimental import pallas as pl
from jax.experimental.pallas import tpu as pltpu
from jax.sharding import PartitionSpec as P

MEANROWS = 256
MESH = pl.DeviceIdType.MESH
RING = 4
MID_CAP = 8
OWN_CAP = 3
ROWS = 16
LANES = 128
FIRST_SPLIT = (4, 4, 2)
OTHER_SPLIT = (2, 2)


def lanes_of(shape):
    return lax.broadcasted_iota(jnp.int32, shape, 1)


def shifted(values, amount):
    return jnp.where(lanes_of(values.shape) >= amount, pltpu.roll(values, amount, axis=1), 0)


def before(mask):
    total = mask
    step = 1
    while step < LANES:
        total = total + shifted(total, step)
        step *= 2
    return total - mask


def rows_sum(values):
    return jnp.broadcast_to(jnp.sum(values, axis=1, keepdims=True), values.shape)


def tall(values, rows):
    return jnp.broadcast_to(values[0:1, :], (rows, LANES))


def route_kernel(pieces, nb, blk, width, n_dp, n_clus, cl_own, mq, *refs):
    labels, pts, queries, ids = refs[:4]
    out, place, train = refs[4:7]
    scratch = refs[7:]
    steps = len(pieces)
    total = 2 * steps
    half = blk // 2
    got1, pack2, got2, pack3 = (scratch[i * total:(i + 1) * total] for i in range(4))
    (
        s1, r1, s2, r2, s3, r3, own,
        mine, got_x, got_y, ring_label, got_r, row_label, got_d,
        tab_a, tab_b, tab_c, tab_d, sm_a, sm_b, sm_c, sm_d,
        sx, rx, sy, ry, sr, rr, sd, rd, tsem,
        q_dp, q_a, q_b, q_a2, q_b2, sq0, rq0, sqa1, rqa1, sqb1, rqb1, sqa2, rqa2, sqb2, rqb2, sq3, rq3,
        picked,
    ) = scratch[4 * total:]
    dp = lax.axis_index("dp")
    cl = lax.axis_index("clus")
    y, x = lax.div(cl, RING), lax.rem(cl, RING)
    core = lax.rem(dp, 2)
    clus_bits = n_clus.bit_length() - 1
    own_bits = cl_own.bit_length() - 1

    def along_x(delta):
        at = lax.rem(x + delta, RING)
        return at, (dp, y * RING + at)

    def along_y(delta):
        at = lax.rem(y + delta, RING)
        return at, (dp, at * RING + x)

    def peer(cls, stage, delta):
        return along_x(delta) if (cls == 0) == (stage == 1) else along_y(delta)

    def row_peer(delta):
        at = lax.rem(dp + delta, n_dp)
        return at, (at, cl)

    def send(src, dst, send_sem, recv_sem, device):
        return pltpu.make_async_remote_copy(
            src_ref=src, dst_ref=dst, send_sem=send_sem, recv_sem=recv_sem, device_id=device, device_id_type=MESH
        )

    barrier = pltpu.get_barrier_semaphore()
    friends = [along_x(d)[1] for d in range(1, RING)] + [along_y(d)[1] for d in range(1, RING)]
    friends += [row_peer(d)[1] for d in range(1, n_dp)]
    for friend in friends:
        pl.semaphore_signal(barrier, inc=1, device_id=friend, device_id_type=MESH)

    lane8 = lanes_of((8, LANES))
    vector = jnp.zeros((8, LANES), jnp.int32)
    for j in range(nb):
        vector = jnp.where(lane8 == cl * nb + j, labels[j, 0] + 1, vector)
    mine[...] = vector

    pl.semaphore_wait(barrier, len(friends))

    def spot(step, cls):
        row0, c0, wide = pieces[step]
        return pl.ds(row0 + cls * half, ROWS), pl.ds(c0, wide)

    def copies1(step, cls):
        q = 2 * step + cls
        rows, cols = spot(step, cls)
        me = x if cls == 0 else y
        return [
            send(pts.at[:, rows, cols], got1[q].at[pl.ds(me * nb, nb)], s1.at[q, d - 1], r1.at[q, d - 1], peer(cls, 1, d)[1])
            for d in range(1, RING)
        ]

    def copies2(step, cls):
        q = 2 * step + cls
        me = y if cls == 0 else x
        made = []
        for d in range(1, RING):
            at, device = peer(cls, 2, d)
            made.append(
                send(
                    pack2[q].at[pl.ds(at * MID_CAP, MID_CAP)],
                    got2[q].at[pl.ds(me * MID_CAP, MID_CAP)],
                    s2.at[q, d - 1], r2.at[q, d - 1], device,
                )
            )
        return made

    def copies3(step, cls):
        q = 2 * step + cls
        rows, cols = spot(step, cls)
        made = []
        for d in range(1, n_dp):
            at, device = row_peer(d)
            made.append(
                send(
                    pack3[q].at[pl.ds(at * OWN_CAP, OWN_CAP)],
                    out.at[pl.ds(dp * OWN_CAP, OWN_CAP), rows, cols],
                    s3.at[q, d - 1], r3.at[q, d - 1], device,
                )
            )
        return made

    def own_copy(step, cls):
        q = 2 * step + cls
        rows, cols = spot(step, cls)
        return pltpu.make_async_copy(
            pack3[q].at[pl.ds(dp * OWN_CAP, OWN_CAP)], out.at[pl.ds(dp * OWN_CAP, OWN_CAP), rows, cols], own.at[q]
        )

    def labels_x():
        return [send(mine, got_x.at[d - 1], sx.at[d - 1], rx.at[d - 1], along_x(d)[1]) for d in range(1, RING)]

    def labels_y():
        return [send(mine, got_y.at[d - 1], sy.at[d - 1], ry.at[d - 1], along_y(d)[1]) for d in range(1, RING)]

    def labels_r():
        return [send(ring_label, got_r.at[d - 1], sr.at[d - 1], rr.at[d - 1], along_y(d)[1]) for d in range(1, RING)]

    def labels_d():
        return [send(row_label, got_d.at[d - 1], sd.at[d - 1], rd.at[d - 1], row_peer(d)[1]) for d in range(1, n_dp)]

    part = width // 2
    quarter = part // 2

    def queries_dp():
        made = []
        for d in range(1, n_dp):
            at, device = row_peer(d)
            cols = pl.ds(pl.multiple_of(lax.rem(at, 2) * part, part), part)
            made.append(send(queries.at[:, cols], q_dp.at[dp], sq0.at[d - 1], rq0.at[d - 1], device))
        return made

    def queries_first():
        a = [
            send(q_dp.at[:, :, pl.ds(0, quarter)], q_a.at[y, x], sqa1.at[d - 1], rqa1.at[d - 1], along_x(d)[1])
            for d in range(1, RING)
        ]
        b = [
            send(q_dp.at[:, :, pl.ds(quarter, quarter)], q_b.at[y, x], sqb1.at[d - 1], rqb1.at[d - 1], along_y(d)[1])
            for d in range(1, RING)
        ]
        return a + b

    def queries_second():
        a = [send(q_a.at[y], q_a.at[y], sqa2.at[d - 1], rqa2.at[d - 1], along_y(d)[1]) for d in range(1, RING)]
        b = [send(q_b.at[:, x], q_b.at[:, x], sqb2.at[d - 1], rqb2.at[d - 1], along_x(d)[1]) for d in range(1, RING)]
        return a + b

    def queries_swap():
        device = (dp + 1 - 2 * core, cl)
        return [
            send(q_a, q_a2, sq3.at[0], rq3.at[0], device),
            send(q_b, q_b2, sq3.at[1], rq3.at[1], device),
        ]

    def start(copies):
        for copy in copies:
            copy.start()

    def start1(step):
        for cls in (0, 1):
            start(copies1(step, cls))

    def own1(step):
        for cls in (0, 1):
            rows, cols = spot(step, cls)
            me = x if cls == 0 else y
            got1[2 * step + cls][pl.ds(me * nb, nb)] = pts[:, rows, cols]

    def columns_of(values):
        return jnp.right_shift(values - 1, own_bits) & (n_clus - 1)

    def tables12():
        for copy in labels_x():
            copy.wait_recv()
        ring_x = mine[...]
        for d in range(1, RING):
            ring_x = ring_x + got_x[d - 1]
        ring_label[...] = ring_x
        for copy in labels_y():
            copy.wait_recv()
        ring_y = mine[...]
        for d in range(1, RING):
            ring_y = ring_y + got_y[d - 1]
        count = RING * MID_CAP
        lane = lanes_of((count, LANES))
        row = lax.broadcasted_iota(jnp.int32, (count, LANES), 0)
        peer_at, slot = jnp.right_shift(row, 3), row & (MID_CAP - 1)
        for tab, values, wanted, index in (
            (tab_a, ring_x, peer_at * RING + x, lane & (RING * nb - 1)),
            (tab_b, ring_y, y * RING + peer_at, jnp.right_shift(lane, 4) * nb + (lane & (nb - 1))),
        ):
            values = tall(values, count)
            hit = ((values > 0) & (columns_of(values) == wanted)).astype(jnp.int32)
            tab[...] = rows_sum(jnp.where((hit > 0) & (before(hit) == slot), index, 0))
        start(labels_r())
        own1(0)
        own1(1)
        for i, (tab, sm) in enumerate(((tab_a, sm_a), (tab_b, sm_b))):
            copy = pltpu.make_async_copy(tab, sm, tsem.at[i])
            copy.start()
            copy.wait()

    def tables3():
        for copy in labels_r():
            copy.wait_recv()
        row_v = ring_label[...]
        for d in range(1, RING):
            row_v = row_v + got_r[d - 1]
        row_label[...] = row_v
        hit = ((row_v > 0) & (columns_of(row_v) == cl)).astype(jnp.int32)
        lane = lane8
        inside = lane & (RING * nb - 1)
        count = hit
        step = 1
        while step < RING * nb:
            count = count + jnp.where(inside >= step, pltpu.roll(count, step, axis=1), 0)
            step *= 2
        at_a = jnp.right_shift(lane, 4) * MID_CAP + count - hit
        earlier = hit
        for step in (RING * nb, 2 * RING * nb):
            earlier = earlier + shifted(earlier, step)
        earlier = earlier - hit
        j = lane & (nb - 1)
        rank = earlier
        for step in range(1, nb):
            rank = rank + jnp.where(j >= step, pltpu.roll(earlier + hit, step, axis=1), 0)
            rank = rank + jnp.where(j < nb - step, pltpu.roll(earlier, LANES - step, axis=1), 0)
        at_b = (jnp.right_shift(lane, 2) & (RING - 1)) * MID_CAP + rank
        count = n_dp * OWN_CAP
        values = tall(row_v, count)
        row = lax.broadcasted_iota(jnp.int32, (count, LANES), 0)
        to_row, slot = row & (n_dp - 1), jnp.right_shift(row, 3)
        row_of = jnp.right_shift(values - 1, own_bits + clus_bits)
        hit = ((values > 0) & (columns_of(values) == cl) & (row_of == to_row)).astype(jnp.int32)
        chosen = (hit > 0) & (before(hit) == slot)
        tab_c[...] = rows_sum(jnp.where(chosen, tall(at_a, count), 0))
        tab_d[...] = rows_sum(jnp.where(chosen, tall(at_b, count), 0))
        start(labels_d())
        for i, (tab, sm) in enumerate(((tab_c, sm_c), (tab_d, sm_d))):
            copy = pltpu.make_async_copy(tab, sm, tsem.at[2 + i])
            copy.start()
            copy.wait()

    def place_slots():
        for copy in labels_d():
            copy.wait_recv()
        sub = lax.broadcasted_iota(jnp.int32, (n_dp, LANES), 0)
        everything = jnp.where(sub == dp, row_label[...], 0)
        for d in range(1, n_dp):
            everything = jnp.where(sub == lax.rem(dp + n_dp - d, n_dp), got_d[d - 1], everything)
        here = dp * n_clus + cl
        hit = ((everything > 0) & (jnp.right_shift(everything - 1, own_bits) == here)).astype(jnp.int32)
        rank = before(hit)
        local = ((everything - 1) & (cl_own - 1)) + 1
        kinds = [rows_sum(jnp.where((hit > 0) & (rank == k), local, 0)) for k in range(OWN_CAP)]
        positions = [jnp.full((n_dp, LANES), -1, jnp.int32) for _ in range(OWN_CAP)]
        base = jnp.zeros((n_dp, LANES), jnp.int32)
        result = jnp.zeros((n_dp, LANES), jnp.int32)
        lane = lanes_of((n_dp, LANES))
        for owned in range(cl_own):
            marks = [(kind == owned + 1).astype(jnp.int32) for kind in kinds]
            per_row = sum(marks[1:], marks[0])
            running = per_row
            step = 1
            while step < n_dp:
                running = running + jnp.where(sub >= step, pltpu.roll(running, step, axis=0), 0)
                step *= 2
            ahead = base + running - per_row
            for k in range(OWN_CAP):
                positions[k] = jnp.where(marks[k] > 0, ahead, positions[k])
                ahead = ahead + marks[k]
            count = jnp.broadcast_to(jnp.sum(per_row, axis=0, keepdims=True), (n_dp, LANES))
            result = jnp.where(lane == OWN_CAP + owned, count, result)
            result = jnp.where(lane == OWN_CAP + cl_own + owned, base, result)
            base = base + jnp.right_shift(count + 1, 1) * 2
        for k in range(OWN_CAP):
            result = jnp.where(lane == k, positions[k], result)
        place[...] = result

    def step12(step):
        for cls in (0, 1):
            q = 2 * step + cls
            mid = y if cls == 0 else x
            for copy in copies1(step, cls):
                copy.wait_recv()
            sm = (sm_a, sm_b)[cls]

            def pack(k, carry, q=q, sm=sm):
                pack2[q][k] = got1[q][sm[k, 0]]
                return carry

            lax.fori_loop(0, RING * MID_CAP, pack, 0, unroll=8)
            start(copies2(step, cls))
            got2[q][pl.ds(mid * MID_CAP, MID_CAP)] = pack2[q][pl.ds(mid * MID_CAP, MID_CAP)]

    def step23(step):
        for cls in (0, 1):
            q = 2 * step + cls
            for copy in copies2(step, cls):
                copy.wait_recv()
            sm = (sm_c, sm_d)[cls]

            def pack(d, carry, q=q, sm=sm):
                for k in range(OWN_CAP):
                    pack3[q][d * OWN_CAP + k] = got2[q][sm[k * n_dp + d, 0]]
                return carry

            lax.fori_loop(0, n_dp, pack, 0, unroll=4)
            start(copies3(step, cls))
            own_copy(step, cls).start()

    def pick_train():
        group = RING * n_dp * queries.shape[0]
        per = queries.shape[0]
        per_bits = per.bit_length() - 1
        row = lax.broadcasted_iota(jnp.int32, (group, mq), 0)
        inner = row & (n_dp * per - 1)
        at_x = jnp.right_shift(row, per_bits + 3)
        stripe = jnp.right_shift(inner, per_bits) * (n_clus * per) + at_x * per + (inner & (per - 1))
        for owned in range(cl_own):
            wanted = jnp.clip(ids[owned:owned + 1, :], 0, n_dp * n_clus * per - 1)

            def add(at_y, carry, owned=owned, wanted=wanted):
                chosen = jnp.where(stripe + at_y * (RING * per) == wanted, 1.0, 0.0).astype(queries.dtype)
                for source, side, which in ((q_a, 0, 0), (q_b, 0, 1), (q_a2, 1, 0), (q_b2, 1, 1)):
                    values = source[at_y].reshape(group, quarter)
                    term = lax.dot_general(
                        chosen, values, (((0,), (0,)), ((), ())), preferred_element_type=jnp.float32
                    )
                    picked[owned, 2 * side + which] += term
                return carry

            lax.fori_loop(0, RING, add, 0)

    start(labels_x())
    start(labels_y())
    start1(0)
    start1(1)
    start(queries_dp())
    q_dp[dp] = queries[:, pl.ds(pl.multiple_of(core * part, part), part)]
    picked[...] = jnp.zeros_like(picked)
    tables12()
    for step in range(steps + 1):
        if step < steps:
            step12(step)
            if step + 2 < steps:
                start1(step + 2)
                own1(step + 2)
        if step == 0:
            tables3()
        if step == 2:
            for copy in queries_dp():
                copy.wait_recv()
            q_a[y, x] = q_dp[:, :, pl.ds(0, quarter)]
            q_b[y, x] = q_dp[:, :, pl.ds(quarter, quarter)]
            start(queries_first())
            place_slots()
        if step == steps - 1:
            for copy in queries_first():
                copy.wait_recv()
            start(queries_second())
        if step >= 1:
            step23(step - 1)
    for copy in queries_second():
        copy.wait_recv()
    start(queries_swap())
    for copy in queries_swap():
        copy.wait_recv()
    pick_train()
    for owned in range(cl_own):
        for which in range(2):
            for side in range(2):
                at = lax.rem(core + side, 2) * part + which * quarter
                train[owned, :, pl.ds(pl.multiple_of(at, quarter), quarter)] = picked[owned, 2 * side + which].astype(
                    train.dtype
                )
    finished = labels_x() + labels_y() + labels_r() + labels_d()
    finished += queries_dp() + queries_first() + queries_second() + queries_swap()
    for step in range(steps):
        for cls in (0, 1):
            finished += copies1(step, cls) + copies2(step, cls)
    for copy in finished:
        copy.wait_send()
    for step in range(steps):
        for cls in (0, 1):
            for copy in copies3(step, cls):
                copy.wait()
            own_copy(step, cls).wait()


def route(points, block_cluster, queries, query_ids, n_dp, n_clus):
    nb, blk, width = points.shape
    cl_own, mq = query_ids.shape
    per = queries.shape[0]
    kind = points.dtype
    pieces = []
    for row0 in range(0, blk // 2, ROWS):
        at = 0
        for part in FIRST_SPLIT if row0 == 0 else OTHER_SPLIT:
            wide = width // part
            pieces.append((row0, at, wide))
            at += wide
    total = 2 * len(pieces)
    dma = pltpu.SemaphoreType.DMA

    def many(count):
        return [pltpu.VMEM((count, ROWS, wide), kind) for _, _, wide in pieces for _ in range(2)]

    def pair(*shape):
        return [dma(shape), dma(shape)]

    def ints(*shape):
        return pltpu.VMEM(shape + (LANES,), jnp.int32)

    mid_rows, own_rows = RING * MID_CAP, n_dp * OWN_CAP
    scratch = many(RING * nb) + many(RING * MID_CAP) * 2 + many(n_dp * OWN_CAP)
    scratch += pair(total, RING - 1) + pair(total, RING - 1) + pair(total, n_dp - 1) + [dma((total,))]
    scratch += [ints(8), ints(RING - 1, 8), ints(RING - 1, 8), ints(8), ints(RING - 1, 8), ints(8), ints(n_dp - 1, 8)]
    scratch += [ints(mid_rows), ints(mid_rows), ints(own_rows), ints(own_rows)]
    scratch += [pltpu.SMEM((rows, LANES), jnp.int32) for rows in (mid_rows, mid_rows, own_rows, own_rows)]
    scratch += pair(RING - 1) * 3 + pair(n_dp - 1) + [dma((4,))]
    quarter = width // 4
    scratch += [pltpu.VMEM((n_dp, per, width // 2), kind)]
    scratch += [pltpu.VMEM((RING, RING, n_dp, per, quarter), kind)] * 4
    scratch += pair(n_dp - 1) + pair(RING - 1) * 4 + pair(2)
    scratch += [pltpu.VMEM((cl_own, 4, mq, quarter), jnp.float32)]
    vmem = pl.BlockSpec(memory_space=pltpu.VMEM)
    return pl.pallas_call(
        functools.partial(route_kernel, pieces, nb, blk, width, n_dp, n_clus, cl_own, mq),
        out_shape=(
            jax.ShapeDtypeStruct((n_dp * OWN_CAP, blk, width), kind),
            jax.ShapeDtypeStruct((n_dp, LANES), jnp.int32),
            jax.ShapeDtypeStruct((cl_own, mq, width), kind),
        ),
        in_specs=[pl.BlockSpec(memory_space=pltpu.SMEM), vmem, vmem, vmem],
        out_specs=(pl.BlockSpec(memory_space=pl.ANY), vmem, vmem),
        scratch_shapes=scratch,
        compiler_params=pltpu.CompilerParams(
            collective_id=0, has_side_effects=True, vmem_limit_bytes=60 * 1024 * 1024
        ),
        name="route",
    )(block_cluster, points, queries, query_ids)


def product_kernel(slots, cl_own, blk, tile, factor, place, blocks, train, gram, cross, sorted_blocks, scores, sem):
    group = pl.program_id(0)
    part = pl.program_id(1)
    step_rows = 2 * blk

    def goal(k):
        return place[lax.div(k, OWN_CAP), lax.rem(k, OWN_CAP)]

    def fetch(k):
        rows = pl.ds(pl.multiple_of(goal(k) * blk, blk), blk)
        return pltpu.make_async_copy(blocks.at[k], sorted_blocks.at[rows], sem.at[k])

    @pl.when((group == 0) & (part == 0))
    def _():
        def begin(k, carry):
            @pl.when(goal(k) >= 0)
            def _():
                fetch(k).start()
            return carry

        lax.fori_loop(0, slots, begin, 0)
        for owned in range(cl_own):
            count = place[0, OWN_CAP + owned]
            end = place[0, OWN_CAP + cl_own + owned] + count

            @pl.when(lax.rem(count, 2) == 1)
            def _():
                sorted_blocks[pl.ds(pl.multiple_of(end * blk, blk), blk), :] = jnp.zeros(
                    (blk, sorted_blocks.shape[1]), sorted_blocks.dtype
                )

        def finish(k, carry):
            @pl.when(goal(k) >= 0)
            def _():
                fetch(k).wait()
            return carry

        lax.fori_loop(0, slots, finish, 0)

    count = place[0, OWN_CAP + group]
    base = place[0, OWN_CAP + cl_own + group]
    steps = lax.div(count + 1, 2)

    def rows_of(step):
        return pl.ds(pl.multiple_of((base + 2 * step) * blk, blk), step_rows)

    @pl.when(part == 0)
    def _():
        def score(step, carry):
            rows = sorted_blocks[rows_of(step), :]
            wide = rows.astype(jnp.float32)
            weight = lax.rsqrt(jnp.mean(wide * wide, axis=1, keepdims=True) + 1e-06)
            raw = lax.dot_general(rows, train[0], (((1,), (1,)), ((), ())), preferred_element_type=jnp.float32)
            scores[pl.ds(pl.multiple_of(step * step_rows, step_rows), step_rows), :] = (raw * weight).astype(scores.dtype)
            return carry

        lax.fori_loop(0, steps, score, 0)

    columns = pl.ds(pl.multiple_of(part * tile, tile), tile)

    def terms(step):
        rows = rows_of(step)
        left = sorted_blocks[rows, columns]
        contract = (((0,), (0,)), ((), ()))
        a = lax.dot_general(left, sorted_blocks[rows, :], contract, preferred_element_type=jnp.float32)
        part_scores = scores[pl.ds(pl.multiple_of(step * step_rows, step_rows), step_rows), :]
        b = lax.dot_general(left, part_scores, contract, preferred_element_type=jnp.float32)
        return a * factor, b * factor

    @pl.when(count == 0)
    def _():
        gram[...] = jnp.zeros_like(gram)
        cross[...] = jnp.zeros_like(cross)

    @pl.when(count > 0)
    def _():
        a, b = terms(0)
        gram[0] = a
        cross[0] = b

        def add(step, carry):
            a, b = terms(step)
            gram[0] += a
            cross[0] += b
            return carry

        lax.fori_loop(1, steps, add, 0)


def products(blocks, place, train):
    slots, blk, width = blocks.shape
    cl_own, mq, _ = train.shape
    tile = 256
    return pl.pallas_call(
        functools.partial(product_kernel, slots, cl_own, blk, tile, 1.0 / MEANROWS),
        out_shape=(
            jax.ShapeDtypeStruct((cl_own, width, width), jnp.float32),
            jax.ShapeDtypeStruct((cl_own, width, mq), jnp.float32),
        ),
        grid_spec=pltpu.PrefetchScalarGridSpec(
            num_scalar_prefetch=1,
            grid=(cl_own, width // tile),
            in_specs=[
                pl.BlockSpec(memory_space=pl.ANY),
                pl.BlockSpec((1, mq, width), lambda g, i, place: (g, 0, 0)),
            ],
            out_specs=(
                pl.BlockSpec((1, tile, width), lambda g, i, place: (g, i, 0)),
                pl.BlockSpec((1, tile, mq), lambda g, i, place: (g, i, 0)),
            ),
            scratch_shapes=[
                pltpu.VMEM(((slots + cl_own) * blk, width), blocks.dtype),
                pltpu.VMEM(((slots + 2) * blk, mq), blocks.dtype),
                pltpu.SemaphoreType.DMA((slots,)),
            ],
        ),
        compiler_params=pltpu.CompilerParams(
            dimension_semantics=("arbitrary", "arbitrary"), vmem_limit_bytes=40 * 1024 * 1024
        ),
        name="products",
    )(place, blocks, train)


def local(points, block_cluster, queries, query_ids):
    own_blocks, place, train = route(
        points, block_cluster, queries, query_ids, lax.axis_size("dp"), lax.axis_size("clus")
    )
    return products(own_blocks, place, train)


def solution(mesh):
    placed = (
        P(("dp", "clus"), None, None),
        P(("dp", "clus"), None),
        P(("dp", "clus"), None),
        P(("dp", "clus"), None),
    )
    return jax.shard_map(
        local,
        mesh=mesh,
        in_specs=placed,
        out_specs=(P(("dp", "clus"), None, None), P(("dp", "clus"), None, None)),
        check_vma=False,
    )
```

time: 200 us -> 127 us (0.64)
  the two profiles are of different devices: /device:TPU:3 before, /device:TPU:1 now
where the time goes in v2:
time: 127 us
  Pallas kernels  120 us (94%)
  local copies, waits for them, and re-layouts  5.81 us (5%)
    pallas_call x1, Pallas kernels, route(): pl.pallas_call(functools.partial(route_kernel, pieces, nb, blk, width, n_...  109 us
    pallas_call x1, Pallas kernels, products(): pl.pallas_call(functools.partial(product_kernel, slots, cl_own, blk, tile...  11.2 us
    unnamed x7, local copies, waits for them, and re-layouts  5.81 us

profile of v2, /device:TPU:1, one launch (start us, length us, event | category | flops | bytes accessed | tf_op | source)
XLA Modules:
  0.0 126.9 jit_solution(16210827614109373972)
XLA Ops:
  0.6 1.3 %copy.6.refs_0_ = s32[4,1]{1,0:T(4,128)} copy(s32[4,1]{0,1:T(1,128)} %param.5) | data formatting | bytes 32 | tf_op args[1]
  1.9 109.2 %route.1 = (bf16[24,128,1024]{2,1,0:T(8,128)(2,1)}, s32[8,128]{1,0:T(8,128)}, bf16[2,128,1024]{2,1,0:T(8,128)(2,1)}) custom-call(s32[4,1]{1,0:T(4,128)} %copy.6.refs_0_, bf16[4,128,1024]{2,1,0:T(8,128)(2,1)} %refs_1_.1, bf16[16,1024]{1,0:T(8,128)(2,1)} %refs_2_.1, s32[2,128]{1,0:T(2,128)} %refs_3_.1), custom_call_target="tpu_custom_call" | custom-call | tf_op jit(solution)/shard_map/route/pallas_call | solution.py:472
  111.2 0.0 copy-start
  111.2 2.8 %copy-done = bf16[24,128,1024]{2,1,0:T(8,128)(2,1)S(1)} copy-done((bf16[24,128,1024]{2,1,0:T(8,128)(2,1)S(1)}, bf16[24,128,1024]{2,1,0:T(8,128)(2,1)}, u32[]{:S(2)}) %copy-start) | copy-done | bytes 6291480
  113.9 0.0 copy-start.1
  113.9 1.0 copy-done.1
  115.0 0.0 copy-start.2
  115.0 0.7 copy-done.2
  115.7 11.2 %products.1 = (f32[2,1024,1024]{2,1,0:T(8,128)}, f32[2,1024,128]{2,1,0:T(8,128)}) custom-call(s32[8,128]{1,0:T(8,128)S(1)} %copy-done.2, bf16[24,128,1024]{2,1,0:T(8,128)(2,1)S(1)} %copy-done, bf16[2,128,1024]{2,1,0:T(8,128)(2,1)S(1)} %copy-done.1), custom_call_target="tpu_custom_call" | custom-call | tf_op jit(solution)/shard_map/products/pallas_call | solution.py:582
Async XLA Ops:
  111.2 2.8 %copy-start = (bf16[24,128,1024]{2,1,0:T(8,128)(2,1)S(1)}, bf16[24,128,1024]{2,1,0:T(8,128)(2,1)}, u32[]{:S(2)}) copy-start(bf16[24,128,1024]{2,1,0:T(8,128)(2,1)} %get-tuple-element.6.blocks) | copy-start | bytes 18874372
  113.9 1.0 copy-start.1
  115.0 0.7 copy-start.2

commit v3 on v2

--- a/solution.py
+++ b/solution.py
@@ -10,12 +10,14 @@
 MEANROWS = 256
 MESH = pl.DeviceIdType.MESH
 RING = 4
+AHEAD = 3
 MID_CAP = 8
 OWN_CAP = 3
 ROWS = 16
 LANES = 128
 FIRST_SPLIT = (4, 4, 2)
 OTHER_SPLIT = (2, 2)
+LAST_SPLIT = (2, 4, 4)
 
 
 def lanes_of(shape):
@@ -95,7 +97,7 @@
     lane8 = lanes_of((8, LANES))
     vector = jnp.zeros((8, LANES), jnp.int32)
     for j in range(nb):
-        vector = jnp.where(lane8 == cl * nb + j, labels[j, 0] + 1, vector)
+        vector = jnp.where(lane8 == cl * nb + j, labels[0, j] + 1, vector)
     mine[...] = vector
 
     pl.semaphore_wait(barrier, len(friends))
@@ -110,8 +112,20 @@
         me = x if cls == 0 else y
         return [
             send(pts.at[:, rows, cols], got1[q].at[pl.ds(me * nb, nb)], s1.at[q, d - 1], r1.at[q, d - 1], peer(cls, 1, d)[1])
-            for d in range(1, RING)
+            for d in (1, RING - 1)
         ]
+
+    def relays1(step, cls):
+        q = 2 * step + cls
+        me = x if cls == 0 else y
+        part = nb // 2
+        made = []
+        for k, d in enumerate((1, RING - 1)):
+            at = pl.ds(lax.rem(me + RING - d, RING) * nb + k * part, part)
+            made.append(
+                send(got1[q].at[at], got1[q].at[at], s1.at[q, 1 + 2 * k], r1.at[q, 1 + 2 * k], peer(cls, 1, d)[1])
+            )
+        return made
 
     def copies2(step, cls):
         q = 2 * step + cls
@@ -185,9 +199,21 @@
         return a + b
 
     def queries_second():
-        a = [send(q_a.at[y], q_a.at[y], sqa2.at[d - 1], rqa2.at[d - 1], along_y(d)[1]) for d in range(1, RING)]
-        b = [send(q_b.at[:, x], q_b.at[:, x], sqb2.at[d - 1], rqb2.at[d - 1], along_x(d)[1]) for d in range(1, RING)]
+        ends = (1, RING - 1)
+        a = [send(q_a.at[y], q_a.at[y], sqa2.at[d - 1], rqa2.at[d - 1], along_y(d)[1]) for d in ends]
+        b = [send(q_b.at[:, x], q_b.at[:, x], sqb2.at[d - 1], rqb2.at[d - 1], along_x(d)[1]) for d in ends]
         return a + b
+
+    def queries_relay():
+        part = RING // 2
+        made = []
+        for k, d in enumerate((1, RING - 1)):
+            some = pl.ds(k * part, part)
+            a = q_a.at[lax.rem(y + RING - d, RING), some]
+            b = q_b.at[some, lax.rem(x + RING - d, RING)]
+            made.append(send(a, a, sqa2.at[1 + 2 * k], rqa2.at[1 + 2 * k], along_y(d)[1]))
+            made.append(send(b, b, sqb2.at[1 + 2 * k], rqb2.at[1 + 2 * k], along_x(d)[1]))
+        return made
 
     def queries_swap():
         device = (dp + 1 - 2 * core, cl)
@@ -203,6 +229,12 @@
     def start1(step):
         for cls in (0, 1):
             start(copies1(step, cls))
+
+    def relay1(step):
+        for cls in (0, 1):
+            for copy in copies1(step, cls):
+                copy.wait_recv()
+            start(relays1(step, cls))
 
     def own1(step):
         for cls in (0, 1):
@@ -225,6 +257,8 @@
         ring_y = mine[...]
         for d in range(1, RING):
             ring_y = ring_y + got_y[d - 1]
+        relay1(0)
+        start(labels_r())
         count = RING * MID_CAP
         lane = lanes_of((count, LANES))
         row = lax.broadcasted_iota(jnp.int32, (count, LANES), 0)
@@ -236,9 +270,14 @@
             values = tall(values, count)
             hit = ((values > 0) & (columns_of(values) == wanted)).astype(jnp.int32)
             tab[...] = rows_sum(jnp.where((hit > 0) & (before(hit) == slot), index, 0))
-        start(labels_r())
-        own1(0)
-        own1(1)
+        relay1(1)
+        for step in range(AHEAD):
+            own1(step)
+        for copy in queries_dp():
+            copy.wait_recv()
+        q_a[y, x] = q_dp[:, :, pl.ds(0, quarter)]
+        q_b[y, x] = q_dp[:, :, pl.ds(quarter, quarter)]
+        start(queries_first())
         for i, (tab, sm) in enumerate(((tab_a, sm_a), (tab_b, sm_b))):
             copy = pltpu.make_async_copy(tab, sm, tsem.at[i])
             copy.start()
@@ -325,7 +364,7 @@
         for cls in (0, 1):
             q = 2 * step + cls
             mid = y if cls == 0 else x
-            for copy in copies1(step, cls):
+            for copy in relays1(step, cls):
                 copy.wait_recv()
             sm = (sm_a, sm_b)[cls]
 
@@ -378,9 +417,9 @@
 
     start(labels_x())
     start(labels_y())
-    start1(0)
-    start1(1)
     start(queries_dp())
+    for step in range(AHEAD):
+        start1(step)
     q_dp[dp] = queries[:, pl.ds(pl.multiple_of(core * part, part), part)]
     picked[...] = jnp.zeros_like(picked)
     tables12()
@@ -388,26 +427,28 @@
         if step < steps:
             step12(step)
             if step + 2 < steps:
-                start1(step + 2)
-                own1(step + 2)
+                relay1(step + 2)
+            if step + AHEAD < steps:
+                start1(step + AHEAD)
+                own1(step + AHEAD)
         if step == 0:
             tables3()
         if step == 2:
-            for copy in queries_dp():
-                copy.wait_recv()
-            q_a[y, x] = q_dp[:, :, pl.ds(0, quarter)]
-            q_b[y, x] = q_dp[:, :, pl.ds(quarter, quarter)]
-            start(queries_first())
             place_slots()
-        if step == steps - 1:
+        if step == steps - 5:
             for copy in queries_first():
                 copy.wait_recv()
             start(queries_second())
+        if step == steps - 4:
+            for copy in queries_second():
+                copy.wait_recv()
+            start(queries_relay())
+        if step == steps - 2:
+            for copy in queries_relay():
+                copy.wait_recv()
+            start(queries_swap())
         if step >= 1:
             step23(step - 1)
-    for copy in queries_second():
-        copy.wait_recv()
-    start(queries_swap())
     for copy in queries_swap():
         copy.wait_recv()
     pick_train()
@@ -419,10 +460,10 @@
                     train.dtype
                 )
     finished = labels_x() + labels_y() + labels_r() + labels_d()
-    finished += queries_dp() + queries_first() + queries_second() + queries_swap()
+    finished += queries_dp() + queries_first() + queries_second() + queries_relay() + queries_swap()
     for step in range(steps):
         for cls in (0, 1):
-            finished += copies1(step, cls) + copies2(step, cls)
+            finished += copies1(step, cls) + relays1(step, cls) + copies2(step, cls)
     for copy in finished:
         copy.wait_send()
     for step in range(steps):
@@ -440,7 +481,8 @@
     pieces = []
     for row0 in range(0, blk // 2, ROWS):
         at = 0
-        for part in FIRST_SPLIT if row0 == 0 else OTHER_SPLIT:
+        last = row0 + ROWS == blk // 2
+        for part in FIRST_SPLIT if row0 == 0 else LAST_SPLIT if last else OTHER_SPLIT:
             wide = width // part
             pieces.append((row0, at, wide))
             at += wide
@@ -458,7 +500,7 @@
 
     mid_rows, own_rows = RING * MID_CAP, n_dp * OWN_CAP
     scratch = many(RING * nb) + many(RING * MID_CAP) * 2 + many(n_dp * OWN_CAP)
-    scratch += pair(total, RING - 1) + pair(total, RING - 1) + pair(total, n_dp - 1) + [dma((total,))]
+    scratch += pair(total, RING) + pair(total, RING - 1) + pair(total, n_dp - 1) + [dma((total,))]
     scratch += [ints(8), ints(RING - 1, 8), ints(RING - 1, 8), ints(8), ints(RING - 1, 8), ints(8), ints(n_dp - 1, 8)]
     scratch += [ints(mid_rows), ints(mid_rows), ints(own_rows), ints(own_rows)]
     scratch += [pltpu.SMEM((rows, LANES), jnp.int32) for rows in (mid_rows, mid_rows, own_rows, own_rows)]
@@ -466,7 +508,7 @@
     quarter = width // 4
     scratch += [pltpu.VMEM((n_dp, per, width // 2), kind)]
     scratch += [pltpu.VMEM((RING, RING, n_dp, per, quarter), kind)] * 4
-    scratch += pair(n_dp - 1) + pair(RING - 1) * 4 + pair(2)
+    scratch += pair(n_dp - 1) + pair(RING - 1) * 2 + pair(RING) * 2 + pair(2)
     scratch += [pltpu.VMEM((cl_own, 4, mq, quarter), jnp.float32)]
     vmem = pl.BlockSpec(memory_space=pltpu.VMEM)
     return pl.pallas_call(
@@ -483,7 +525,7 @@
             collective_id=0, has_side_effects=True, vmem_limit_bytes=60 * 1024 * 1024
         ),
         name="route",
-    )(block_cluster, points, queries, query_ids)
+    )(block_cluster.reshape(1, nb), points, queries, query_ids)
 
 
 def product_kernel(slots, cl_own, blk, tile, factor, place, blocks, train, gram, cross, sorted_blocks, scores, sem):
@@ -603,7 +645,7 @@
             ],
         ),
         compiler_params=pltpu.CompilerParams(
-            dimension_semantics=("arbitrary", "arbitrary"), vmem_limit_bytes=40 * 1024 * 1024
+            dimension_semantics=("arbitrary", "arbitrary"), vmem_limit_bytes=60 * 1024 * 1024
         ),
         name="products",
     )(place, blocks, train)

time: 127 us -> 124 us (0.976)
  the two profiles are of different devices: /device:TPU:1 before, /device:TPU:3 now
where the time goes in v3:
time: 124 us
  Pallas kernels  123 us (99%)
    pallas_call x1, Pallas kernels, route(): pl.pallas_call(functools.partial(route_kernel, pieces, nb, blk, width, n_...  105 us
    pallas_call x1, Pallas kernels, products(): pl.pallas_call(functools.partial(product_kernel, slots, cl_own, blk, tile...  18 us

profile of v3, /device:TPU:3, one launch (start us, length us, event | category | flops | bytes accessed | tf_op | source)
XLA Modules:
  0.0 123.7 jit_solution(14644193556859660930)
XLA Ops:
  0.6 105.0 %route.1 = (bf16[24,128,1024]{2,1,0:T(8,128)(2,1)}, s32[8,128]{1,0:T(8,128)}, bf16[2,128,1024]{2,1,0:T(8,128)(2,1)}) custom-call(s32[1,4]{1,0:T(1,128)} %bitcast.1, bf16[4,128,1024]{2,1,0:T(8,128)(2,1)} %refs_1_.1, bf16[16,1024]{1,0:T(8,128)(2,1)} %refs_2_.1, s32[2,128]{1,0:T(2,128)} %refs_3_.1), custom_call_target="tpu_custom_call" | custom-call | tf_op jit(solution)/shard_map/route/pallas_call | solution.py:514
  105.7 18.0 %products.1 = (f32[2,1024,1024]{2,1,0:T(8,128)}, f32[2,1024,128]{2,1,0:T(8,128)}) custom-call(s32[8,128]{1,0:T(8,128)} %get-tuple-element.5.place, bf16[24,128,1024]{2,1,0:T(8,128)(2,1)} %get-tuple-element.6.blocks, bf16[2,128,1024]{2,1,0:T(8,128)(2,1)} %get-tuple-element.7.train), custom_call_target="tpu_custom_call" | custom-call | tf_op jit(solution)/shard_map/products/pallas_call | solution.py:624

commit v4 on v3

--- a/solution.py
+++ b/solution.py
@@ -15,7 +15,7 @@
 OWN_CAP = 3
 ROWS = 16
 LANES = 128
-FIRST_SPLIT = (4, 4, 2)
+FIRST_SPLIT = (8, 8, 4, 2)
 OTHER_SPLIT = (2, 2)
 LAST_SPLIT = (2, 4, 4)
 
@@ -244,6 +244,15 @@
 
     def columns_of(values):
         return jnp.right_shift(values - 1, own_bits) & (n_clus - 1)
+
+    def to_scalars(at, first, first_out, second, second_out):
+        copies = [
+            pltpu.make_async_copy(first, first_out, tsem.at[at]),
+            pltpu.make_async_copy(second, second_out, tsem.at[at + 1]),
+        ]
+        start(copies)
+        for copy in copies:
+            copy.wait()
 
     def tables12():
         for copy in labels_x():
@@ -273,15 +282,7 @@
         relay1(1)
         for step in range(AHEAD):
             own1(step)
-        for copy in queries_dp():
-            copy.wait_recv()
-        q_a[y, x] = q_dp[:, :, pl.ds(0, quarter)]
-        q_b[y, x] = q_dp[:, :, pl.ds(quarter, quarter)]
-        start(queries_first())
-        for i, (tab, sm) in enumerate(((tab_a, sm_a), (tab_b, sm_b))):
-            copy = pltpu.make_async_copy(tab, sm, tsem.at[i])
-            copy.start()
-            copy.wait()
+        to_scalars(0, tab_a, sm_a, tab_b, sm_b)
 
     def tables3():
         for copy in labels_r():
@@ -319,10 +320,7 @@
         tab_c[...] = rows_sum(jnp.where(chosen, tall(at_a, count), 0))
         tab_d[...] = rows_sum(jnp.where(chosen, tall(at_b, count), 0))
         start(labels_d())
-        for i, (tab, sm) in enumerate(((tab_c, sm_c), (tab_d, sm_d))):
-            copy = pltpu.make_async_copy(tab, sm, tsem.at[2 + i])
-            copy.start()
-            copy.wait()
+        to_scalars(2, tab_c, sm_c, tab_d, sm_d)
 
     def place_slots():
         for copy in labels_d():
@@ -426,15 +424,21 @@
     for step in range(steps + 1):
         if step < steps:
             step12(step)
-            if step + 2 < steps:
-                relay1(step + 2)
-            if step + AHEAD < steps:
-                start1(step + AHEAD)
-                own1(step + AHEAD)
+        if step >= 1:
+            step23(step - 1)
+        if step + 2 < steps:
+            relay1(step + 2)
+        if step + AHEAD < steps:
+            start1(step + AHEAD)
+            own1(step + AHEAD)
         if step == 0:
             tables3()
-        if step == 2:
-            place_slots()
+        if step == 1:
+            for copy in queries_dp():
+                copy.wait_recv()
+            q_a[y, x] = q_dp[:, :, pl.ds(0, quarter)]
+            q_b[y, x] = q_dp[:, :, pl.ds(quarter, quarter)]
+            start(queries_first())
         if step == steps - 5:
             for copy in queries_first():
                 copy.wait_recv()
@@ -443,12 +447,12 @@
             for copy in queries_second():
                 copy.wait_recv()
             start(queries_relay())
+        if step == steps - 3:
+            place_slots()
         if step == steps - 2:
             for copy in queries_relay():
                 copy.wait_recv()
             start(queries_swap())
-        if step >= 1:
-            step23(step - 1)
     for copy in queries_swap():
         copy.wait_recv()
     pick_train()
@@ -588,33 +592,42 @@
 
     columns = pl.ds(pl.multiple_of(part * tile, tile), tile)
 
-    def terms(step):
-        rows = rows_of(step)
+    def terms(step, some):
+        rows = pl.ds(pl.multiple_of((base + 2 * step) * blk, blk), some)
         left = sorted_blocks[rows, columns]
         contract = (((0,), (0,)), ((), ()))
         a = lax.dot_general(left, sorted_blocks[rows, :], contract, preferred_element_type=jnp.float32)
-        part_scores = scores[pl.ds(pl.multiple_of(step * step_rows, step_rows), step_rows), :]
+        part_scores = scores[pl.ds(pl.multiple_of(step * step_rows, step_rows), some), :]
         b = lax.dot_general(left, part_scores, contract, preferred_element_type=jnp.float32)
         return a * factor, b * factor
+
+    odd = lax.rem(steps, 2)
+
+    def first(some):
+        a, b = terms(0, some)
+        gram[0] = a
+        cross[0] = b
 
     @pl.when(count == 0)
     def _():
         gram[...] = jnp.zeros_like(gram)
         cross[...] = jnp.zeros_like(cross)
 
-    @pl.when(count > 0)
+    @pl.when(odd == 1)
     def _():
-        a, b = terms(0)
-        gram[0] = a
-        cross[0] = b
-
-        def add(step, carry):
-            a, b = terms(step)
-            gram[0] += a
-            cross[0] += b
-            return carry
-
-        lax.fori_loop(1, steps, add, 0)
+        first(step_rows)
+
+    @pl.when((count > 0) & (odd == 0))
+    def _():
+        first(2 * step_rows)
+
+    def add(pair, carry):
+        a, b = terms(2 * pair + odd, 2 * step_rows)
+        gram[0] += a
+        cross[0] += b
+        return carry
+
+    lax.fori_loop(1 - odd, lax.div(steps, 2), add, 0)
 
 
 def products(blocks, place, train):

time: 124 us -> 121 us (0.976); the launches traced: 124 us -> 119 us
  Pallas kernels: 123 us -> 118 us
    pallas_call x1, Pallas kernels: 18 us -> 11.6 us  [products(): pl.pallas_call(functools.partial(product_kernel, slots, cl_own, blk, tile...]
    pallas_call x1, Pallas kernels: 105 us -> 106 us  [route(): pl.pallas_call(functools.partial(route_kernel, pieces, nb, blk, width, n_...]
where the time goes in v4:
time: 121 us; the launch traced here: 119 us
  Pallas kernels  118 us (98%)
    pallas_call x1, Pallas kernels, route(): pl.pallas_call(functools.partial(route_kernel, pieces, nb, blk, width, n_...  106 us
    pallas_call x1, Pallas kernels, products(): pl.pallas_call(functools.partial(product_kernel, slots, cl_own, blk, tile...  11.6 us

profile of v4, /device:TPU:3, one launch (start us, length us, event | category | flops | bytes accessed | tf_op | source)
XLA Modules:
  0.0 118.6 jit_solution(13012073641895703899)
XLA Ops:
  0.6 106.4 %route.1 = (bf16[24,128,1024]{2,1,0:T(8,128)(2,1)}, s32[8,128]{1,0:T(8,128)}, bf16[2,128,1024]{2,1,0:T(8,128)(2,1)}) custom-call(s32[1,4]{1,0:T(1,128)} %bitcast.1, bf16[4,128,1024]{2,1,0:T(8,128)(2,1)} %refs_1_.1, bf16[16,1024]{1,0:T(8,128)(2,1)} %refs_2_.1, s32[2,128]{1,0:T(2,128)} %refs_3_.1), custom_call_target="tpu_custom_call" | custom-call | tf_op jit(solution)/shard_map/route/pallas_call | solution.py:518
  107.0 11.6 %products.1 = (f32[2,1024,1024]{2,1,0:T(8,128)}, f32[2,1024,128]{2,1,0:T(8,128)}) custom-call(s32[8,128]{1,0:T(8,128)} %get-tuple-element.5.place, bf16[24,128,1024]{2,1,0:T(8,128)(2,1)} %get-tuple-element.6.blocks, bf16[2,128,1024]{2,1,0:T(8,128)(2,1)} %get-tuple-element.7.train), custom_call_target="tpu_custom_call" | custom-call | tf_op jit(solution)/shard_map/products/pallas_call | solution.py:637

commit v5 on v4

--- a/solution.py
+++ b/solution.py
@@ -16,7 +16,7 @@
 ROWS = 16
 LANES = 128
 FIRST_SPLIT = (8, 8, 4, 2)
-OTHER_SPLIT = (2, 2)
+OTHER_SPLIT = (4, 4, 4, 4)
 LAST_SPLIT = (2, 4, 4)
 
 

time: 121 us -> 124 us (1.025)
  the two profiles are of different devices: /device:TPU:3 before, /device:TPU:37 now
where the time goes in v5:
time: 124 us; the launch traced here: 123 us
  Pallas kernels  123 us (99%)
    pallas_call x1, Pallas kernels, route(): pl.pallas_call(functools.partial(route_kernel, pieces, nb, blk, width, n_...  109 us
    pallas_call x1, Pallas kernels, products(): pl.pallas_call(functools.partial(product_kernel, slots, cl_own, blk, tile...  13.9 us

profile of v5, /device:TPU:37, one launch (start us, length us, event | category | flops | bytes accessed | tf_op | source)
XLA Modules:
  0.0 123.4 jit_solution(2113159281716103249)
XLA Ops:
  0.6 108.9 %route.1 = (bf16[24,128,1024]{2,1,0:T(8,128)(2,1)}, s32[8,128]{1,0:T(8,128)}, bf16[2,128,1024]{2,1,0:T(8,128)(2,1)}) custom-call(s32[1,4]{1,0:T(1,128)} %bitcast.1, bf16[4,128,1024]{2,1,0:T(8,128)(2,1)} %refs_1_.1, bf16[16,1024]{1,0:T(8,128)(2,1)} %refs_2_.1, s32[2,128]{1,0:T(2,128)} %refs_3_.1), custom_call_target="tpu_custom_call" | custom-call | tf_op jit(solution)/shard_map/route/pallas_call | solution.py:518
  109.6 13.9 %products.1 = (f32[2,1024,1024]{2,1,0:T(8,128)}, f32[2,1024,128]{2,1,0:T(8,128)}) custom-call(s32[8,128]{1,0:T(8,128)} %get-tuple-element.5.place, bf16[24,128,1024]{2,1,0:T(8,128)(2,1)} %get-tuple-element.6.blocks, bf16[2,128,1024]{2,1,0:T(8,128)(2,1)} %get-tuple-element.7.train), custom_call_target="tpu_custom_call" | custom-call | tf_op jit(solution)/shard_map/products/pallas_call | solution.py:637
